TPU v7x, 256 devices: a whole 4x4x8 slice. The times are simulated.
256 devices in a mesh: dp: 8 (over y, core), seq: 32 (over z, x).
Axes of the slice: x: 4, y: 4, z: 8, core: 2. Of those that a mesh axis runs over, the one named last changes fastest.
Arguments:
- queries: bfloat16 [8, 16384, 1024], P('dp', 'seq'), may hold values from -6 to 6
- keys: bfloat16 [8, 16384, 1024], P('dp', 'seq'), may hold values from -6 to 6
- values: bfloat16 [8, 16384, 1024], P('dp', 'seq'), may hold values from -6 to 6
- out_grad: bfloat16 [8, 16384, 2048], P('dp', 'seq'), may hold values from -6 to 6
- out_weight: bfloat16 [1024, 2048], P(('dp', 'seq')), may hold values from -0.125 to 0.125
- gain: float32 [1024], replicated, may hold values from 0.1 to 1.9
Outputs:
- query_grad: bfloat16 [8, 16384, 1024], P('dp', 'seq')
- key_grad: bfloat16 [8, 16384, 1024], P('dp', 'seq')
- value_grad: bfloat16 [8, 16384, 1024], P('dp', 'seq')
- weight_grad: float32 [1024, 2048], P(('dp', 'seq'))
- gain_grad: float32 [1024], replicated
All inputs are finite; a program needn't handle non-finite values.
Results may differ from a plain program's by a relative error of at most 0.015.
Values may be sent and summed in bfloat16 or wider, within the bound.
A program may use at most 128 MiB of HBM per device.

v0:
```python
import jax
import jax.numpy as jnp
from jax import lax
from jax.sharding import PartitionSpec as P

HEADS = 8
HEAD_DIM = 128
BLOCK = 512
HD = 1024
norm_eps = 1e-06


def prefix(x, axis, combine, identity, reverse):
    peers, here = (lax.axis_size(axis), lax.axis_index(axis))
    everything = lax.all_gather(x, axis)
    start = jnp.broadcast_to(jnp.asarray(identity, x.dtype), x.shape)

    def hop(k, before):
        at = peers - 1 - k if reverse else k
        reached = at > here if reverse else at < here
        new = combine(before, everything[at])
        return jnp.where(reached, new, before)

    return lax.fori_loop(0, peers, hop, start)


def causal_mask():
    places = jnp.arange(BLOCK, dtype=jnp.int32)
    return (places[None, :] <= places[:, None]).astype(jnp.float32)


def add_states(earlier, later):
    return earlier + later


def before_each(block_terms):
    running = jnp.cumsum(block_terms, axis=0)
    return jnp.concatenate([jnp.zeros_like(block_terms), running[:-1]], axis=0)


def after_each(block_terms):
    running = jnp.cumsum(block_terms[::-1], axis=0)[::-1]
    return jnp.concatenate([running[1:], jnp.zeros_like(block_terms)], axis=0)


def shards(queries, keys, values, out_grad, out_weight, gain):
    tok_count = queries.shape[1]
    blocks = tok_count // BLOCK
    block_shape = (blocks, BLOCK, HEADS, HEAD_DIM)
    query_blk = queries.reshape(block_shape)
    key_blk = keys.reshape(block_shape)
    value_blk = values.reshape(block_shape)
    grad_rows = out_grad[0]
    gain_heads = gain.reshape(HEADS, HEAD_DIM)
    causal = causal_mask()
    state_zero = jnp.zeros((HEADS, HEAD_DIM, HEAD_DIM), jnp.float32)
    block_kv = jnp.einsum("nshd,nshe->nhde", key_blk, value_blk, preferred_element_type=jnp.float32)
    within = before_each(block_kv)
    local_total = jnp.sum(block_kv, axis=0)
    before = prefix(local_total, "seq", add_states, state_zero, False)
    state_bf = (before[None] + within).astype(jnp.bfloat16)
    scores = jnp.einsum("nthd,nshd->nhts", query_blk, key_blk, preferred_element_type=jnp.float32)
    attn_bf = (scores * causal[None, None]).astype(jnp.bfloat16)
    outputs = jnp.einsum("nhts,nshd->nthd", attn_bf, value_blk, preferred_element_type=jnp.float32)
    outputs = outputs + jnp.einsum(
        "nthd,nhde->nthe", query_blk, state_bf, preferred_element_type=jnp.float32
    )
    rms = jnp.sqrt(jnp.mean(outputs * outputs, axis=-1, keepdims=True) + norm_eps)
    normed = outputs / rms
    unit_bf = (normed * gain_heads[None, None]).astype(jnp.bfloat16)
    unit_grad = lax.dot_general(
        grad_rows,
        lax.all_gather(out_weight, ("dp", "seq"), axis=0, tiled=True),
        (((1,), (1,)), ((), ())),
        preferred_element_type=jnp.float32,
    ).reshape(block_shape)
    gain_part = jnp.sum(unit_grad * normed, axis=(0, 1)).reshape(-1)
    scaled = unit_grad * gain_heads[None, None]
    middle = jnp.mean(scaled * normed, axis=-1, keepdims=True)
    attn_grad = ((scaled - normed * middle) / rms).astype(jnp.bfloat16)
    block_qg = jnp.einsum(
        "nthd,nthe->nhde", query_blk, attn_grad, preferred_element_type=jnp.float32
    )
    later_inside = after_each(block_qg)
    local_qg = jnp.sum(block_qg, axis=0)
    after = prefix(local_qg, "seq", add_states, state_zero, True)
    rev_bf = (after[None] + later_inside).astype(jnp.bfloat16)
    score_grad = (
        jnp.einsum("nthe,nshe->nhts", attn_grad, value_blk, preferred_element_type=jnp.float32)
        * causal[None, None]
    ).astype(jnp.bfloat16)
    query_g = jnp.einsum("nhts,nshd->nthd", score_grad, key_blk, preferred_element_type=jnp.float32)
    query_g = query_g + jnp.einsum(
        "nthe,nhde->nthd", attn_grad, state_bf, preferred_element_type=jnp.float32
    )
    key_g = jnp.einsum("nhts,nthd->nshd", score_grad, query_blk, preferred_element_type=jnp.float32)
    key_g = key_g + jnp.einsum(
        "nshe,nhde->nshd", value_blk, rev_bf, preferred_element_type=jnp.float32
    )
    value_g = jnp.einsum("nhts,nthe->nshe", attn_bf, attn_grad, preferred_element_type=jnp.float32)
    value_g = value_g + jnp.einsum(
        "nshd,nhde->nshe", key_blk, rev_bf, preferred_element_type=jnp.float32
    )
    unit_flat = unit_bf.reshape(tok_count, HD)
    data_count = lax.axis_size("dp")
    seq_count = lax.axis_size("seq")
    weight_sum = lax.psum_scatter(
        lax.dot_general(
            unit_flat, grad_rows, (((0,), (0,)), ((), ())), preferred_element_type=jnp.float32
        ),
        ("dp", "seq"),
        scatter_dimension=0,
        tiled=True,
    )
    gain_total = lax.psum(gain_part, ("dp", "seq"))
    factor = 1.0 / jnp.sqrt(jnp.float32(tok_count * data_count * seq_count))
    out_shape = (1, tok_count, HD)
    return (
        query_g.astype(jnp.bfloat16).reshape(out_shape),
        key_g.astype(jnp.bfloat16).reshape(out_shape),
        value_g.astype(jnp.bfloat16).reshape(out_shape),
        weight_sum * factor,
        gain_total * factor,
    )


def solution(mesh):
    placed = (
        P("dp", "seq", None),
        P("dp", "seq", None),
        P("dp", "seq", None),
        P("dp", "seq", None),
        P(("dp", "seq"), None),
        P(),
    )
    return jax.shard_map(
        shards,
        mesh=mesh,
        in_specs=placed,
        out_specs=(
            P("dp", "seq", None),
            P("dp", "seq", None),
            P("dp", "seq", None),
            P(("dp", "seq"), None),
            P(),
        ),
        check_vma=False,
    )
```

profile of v0, /device:TPU:1, one launch (start us, length us, event | category | flops | bytes accessed | tf_op | source)
XLA Modules:
  0.0 829.1 jit_solution(12613035057772357722)
XLA Ops:
  16.8 3.3 multiply_convert_fusion.1
  20.1 111.6 %all-gather.11.cloned.1.call-done = bf16[256,4,2048]{2,1,0:T(4,128)(2,1)} async-done(((bf16[1,4,2048]{2,1,0:T(4,128)(2,1)}), bf16[256,4,2048]{2,1,0:T(4,128)(2,1)}) %all-gather.11.cloned.1.call-update) | async-done | bytes 4194320 | tf_op jit(solution)/shard_map/all_gather | solution.py:73
  131.7 6.9 reshape.183
  138.6 5.9 fusion.5
  144.5 126.3 %all-gather.7.cloned.1.call-done = f32[256,128,128]{2,1,0:T(8,128)} async-done(((f32[8,128,128]{2,1,0:T(8,128)}), f32[256,128,128]{2,1,0:T(8,128)}) %all-gather.7.cloned.1.call-update) | async-done | bytes 16777232 | tf_op jit(solution)/shard_map/all_gather | solution.py:15
  270.8 65.3 %while.30 = (s32[]{:T(128)}, f32[8,128,128]{2,1,0:T(8,128)}, s32[]{:T(128)}, f32[32,8,128,128]{3,2,1,0:T(8,128)}, s32[]{:T(128)}, /*index=5*/s32[]{:T(128)}) while((s32[]{:T(128)}, f32[8,128,128]{2,1,0:T(8,128)}, s32[]{:T(128)}, f32[32,8,128,128]{3,2,1,0:T(8,128)}, s32[]{:T(128)}, /*index=5*/s32[]{:T(128)}) %tuple.92), condition=%wide.region_1.2_spmd.clone, body=%wide.region_0.0_spmd.clone.sunk | while | flops 393220 | bytes 1572957 | solution.py:24
  278.8 2.0 add_select_fusion.4
  280.9 2.0 add_select_fusion.4
  282.9 2.0 add_select_fusion.4
  285.0 2.0 add_select_fusion.4
  293.1 2.0 add_select_fusion.4
  338.0 3.8 fusion.2
  344.3 5.6 fusion.3
  352.7 2.1 copy.47
  357.8 2.5 fusion.1
  360.2 2.3 copy.52
  362.5 76.0 %psum.7 = f32[1024]{0:T(1024)S(1)} all-reduce(f32[1024]{0:T(1024)S(1)} %bitcast.111), channel_id=1, replica_groups=mesh['dp'=8,'seq'=32] {'dp','seq'}, use_global_device_ids=true, to_apply=%region_8.9 | all-reduce | flops 1024 | bytes 8192 | tf_op jit(solution)/shard_map/psum | solution.py:115
  439.1 4.3 fusion.7
  443.4 183.4 %all-reduce.3.cloned.1.call-done = f32[1024,2048]{1,0:T(8,128)} async-done(((f32[1024,2048]{1,0:T(8,128)}), f32[1024,2048]{1,0:T(8,128)}) %all-reduce.3.cloned.1.call-update) | async-done | bytes 8388624
  628.2 140.6 %all-gather.9.cloned.1.call-done = f32[256,128,128]{2,1,0:T(8,128)} async-done(((f32[8,128,128]{2,1,0:T(8,128)}), f32[256,128,128]{2,1,0:T(8,128)}) %all-gather.9.cloned.1.call-update) | async-done | bytes 16777232 | tf_op jit(solution)/shard_map/all_gather | solution.py:15
  768.8 40.2 %while.31 = (s32[]{:T(128)}, f32[8,128,128]{2,1,0:T(8,128)S(1)}, s32[]{:T(128)}, f32[32,8,128,128]{3,2,1,0:T(8,128)}, s32[]{:T(128)}, /*index=5*/s32[]{:T(128)}, s32[]{:T(128)}, s32[]{:T(128)}) while((s32[]{:T(128)}, f32[8,128,128]{2,1,0:T(8,128)S(1)}, s32[]{:T(128)}, f32[32,8,128,128]{3,2,1,0:T(8,128)}, s32[]{:T(128)}, ...), condition=%wide.region_5.6_spmd.clone, body=%wide.region_4.5_spmd.clone.sunk | while | flops 393224 | bytes 1573019 | solution.py:24
  813.2 2.4 copy.54
  815.5 4.8 fusion
  820.3 2.3 copy.53
  (121 shorter events, 120.1 us)
Async XLA Ops:
  7.2 131.5 %copy-start = (bf16[1,512,2048]{2,1,0:T(8,128)(2,1)S(1)}, bf16[1,512,2048]{2,1,0:T(8,128)(2,1)}, u32[]{:S(2)}) copy-start(bf16[1,512,2048]{2,1,0:T(8,128)(2,1)} %param.13) | copy-start | bytes 6291460
  7.2 124.5 %all-gather.11.cloned.1.call-start = ((), (), s32[]{:S(2)}) async-start(), calls=%async_computation.2 | async-start | bytes 4210688 | tf_op jit(solution)/shard_map/all_gather | solution.py:73
  7.9 262.9 %all-gather.7.cloned.1.call-start = ((), (), s32[]{:S(2)}) async-start(), calls=%async_computation | async-start | bytes 17301504 | tf_op jit(solution)/shard_map/all_gather | solution.py:15
  9.5 1.5 copy-start.7
  10.9 1.6 copy-start.12
  13.8 612.9 %all-reduce.3.cloned.1.call-start = ((), (), s32[]{:S(2)}) async-start(), calls=%async_computation.3 | async-start | bytes 16777216
  13.9 2.9 copy-start.8
  15.5 1.0 copy-start.4
  15.6 1.2 copy-start.10
  338.0 3.9 copy-start.15
  338.0 3.9 copy-start.16
  349.9 1.2 copy-start.3
  349.9 1.5 copy-start.5
  349.9 418.8 %all-gather.9.cloned.1.call-start = ((), (), s32[]{:S(2)}) async-start(), calls=%async_computation.1 | async-start | bytes 17301504 | tf_op jit(solution)/shard_map/all_gather | solution.py:15
  354.8 1.6 copy-start.11
  356.4 1.4 copy-start.13
  357.8 2.5 copy-start.2
  809.0 1.8 copy-start.9
  809.0 2.7 copy-start.14
  813.2 2.4 copy-start.6
  815.5 7.0 copy-start.1
Sparse Core Ops, SparseCore 0:
  11.7 119.9 all-gather.10
  134.9 135.9 all-gather.6
  350.1 276.6 all-reduce.2
  629.2 139.5 all-gather.8
where the time goes:
time: 832 us; the launch traced here: 829 us
  waiting for transfers between devices  562 us (68%)
  other arithmetic  109 us (13%)
  blocking collectives  76 us (9%)
  matrix products  40.8 us (5%)
  local copies, waits for them, and re-layouts  25.4 us (3%)
  between operations  14 us (2%)
    all_gather x2, waiting for transfers between devices, prefix(): everything = lax.all_gather(x, axis)  267 us
    unnamed x5, waiting for transfers between devices  184 us
    all_gather x1, waiting for transfers between devices, shards(): lax.all_gather(out_weight, ('dp', 'seq'), axis=0, tiled=True)  112 us
    select_n x64, other arithmetic, hop(): return jnp.where(reached, new, before)  105 us
    psum x1, blocking collectives, shards(): gain_total = lax.psum(gain_part, ('dp', 'seq'))  76 us
    unnamed x41, local copies, waits for them, and re-layouts  21.9 us
  transfers between devices with their start and end apart: 4, of which 4 were waited for; matrix products, arithmetic and copies ran while one was open for 5% of the time, Pallas kernels for 0%

commit v1 on v0

--- a/solution.py
+++ b/solution.py
@@ -112,7 +112,7 @@
         scatter_dimension=0,
         tiled=True,
     )
-    gain_total = lax.psum(gain_part, ("dp", "seq"))
+    gain_total = lax.psum(lax.psum(gain_part, "dp"), "seq")
     factor = 1.0 / jnp.sqrt(jnp.float32(tok_count * data_count * seq_count))
     out_shape = (1, tok_count, HD)
     return (

time: 832 us -> 832 us (level)
    psum x1 -> x2, blocking collectives: 76 us -> 71 us  [shards(): gain_total = lax.psum(lax.psum(gain_part, 'dp'), 'seq')]
where the time goes in v1:
time: 832 us; the launch traced here: 829 us
  waiting for transfers between devices  567 us (68%)
  other arithmetic  110 us (13%)
  blocking collectives  71 us (9%)
  matrix products  40.8 us (5%)
  local copies, waits for them, and re-layouts  25.4 us (3%)
  between operations  14 us (2%)
    all_gather x2, waiting for transfers between devices, prefix(): everything = lax.all_gather(x, axis)  267 us
    unnamed x5, waiting for transfers between devices  189 us
    all_gather x1, waiting for transfers between devices, shards(): lax.all_gather(out_weight, ('dp', 'seq'), axis=0, tiled=True)  112 us
    select_n x64, other arithmetic, hop(): return jnp.where(reached, new, before)  105 us
    psum x2, blocking collectives, shards(): gain_total = lax.psum(lax.psum(gain_part, 'dp'), 'seq')  71 us
    unnamed x41, local copies, waits for them, and re-layouts  21.9 us
  transfers between devices with their start and end apart: 4, of which 4 were waited for; matrix products, arithmetic and copies ran while one was open for 5% of the time, Pallas kernels for 0%

profile of v1, /device:TPU:1, one launch (start us, length us, event | category | flops | bytes accessed | tf_op | source)
XLA Modules:
  0.0 829.2 jit_solution(17557568287463174366)
XLA Ops:
  16.8 3.3 multiply_convert_fusion.1
  20.1 111.6 %all-gather.11.cloned.1.call-done = bf16[256,4,2048]{2,1,0:T(4,128)(2,1)} async-done(((bf16[1,4,2048]{2,1,0:T(4,128)(2,1)}), bf16[256,4,2048]{2,1,0:T(4,128)(2,1)}) %all-gather.11.cloned.1.call-update) | async-done | bytes 4194320 | tf_op jit(solution)/shard_map/all_gather | solution.py:73
  131.7 7.0 reshape.183
  138.7 5.9 fusion.5
  144.5 126.3 %all-gather.7.cloned.1.call-done = f32[256,128,128]{2,1,0:T(8,128)} async-done(((f32[8,128,128]{2,1,0:T(8,128)}), f32[256,128,128]{2,1,0:T(8,128)}) %all-gather.7.cloned.1.call-update) | async-done | bytes 16777232 | tf_op jit(solution)/shard_map/all_gather | solution.py:15
  270.8 65.7 %while.30 = (s32[]{:T(128)}, f32[8,128,128]{2,1,0:T(8,128)}, s32[]{:T(128)}, f32[32,8,128,128]{3,2,1,0:T(8,128)}, s32[]{:T(128)}, /*index=5*/s32[]{:T(128)}) while((s32[]{:T(128)}, f32[8,128,128]{2,1,0:T(8,128)}, s32[]{:T(128)}, f32[32,8,128,128]{3,2,1,0:T(8,128)}, s32[]{:T(128)}, /*index=5*/s32[]{:T(128)}) %tuple.92), condition=%wide.region_1.2_spmd.clone, body=%wide.region_0.0_spmd.clone.sunk | while | flops 393220 | bytes 1572957 | solution.py:24
  276.8 2.1 add_select_fusion.4
  285.1 2.1 add_select_fusion.4
  291.2 2.1 add_select_fusion.4
  293.3 2.1 add_select_fusion.4
  299.5 2.1 add_select_fusion.4
  338.4 3.8 fusion.2
  344.8 5.6 fusion.3
  358.2 2.5 fusion.1
  360.7 2.3 copy.52
  362.9 13.2 %psum.14 = f32[1024]{0:T(1024)S(1)} all-reduce(f32[1024]{0:T(1024)S(1)} %bitcast.111), channel_id=1, replica_groups=mesh['dp'=8,'seq'=32] {'dp'}, use_global_device_ids=true, to_apply=%region_8.9 | all-reduce | flops 1024 | bytes 8192 | tf_op jit(solution)/shard_map/psum | solution.py:115
  376.1 57.8 %psum.15 = f32[1024]{0:T(1024)S(1)} all-reduce(f32[1024]{0:T(1024)S(1)} %psum.14), channel_id=1, replica_groups=mesh['dp'=8,'seq'=32] {'seq'}, use_global_device_ids=true, to_apply=%region_9.10 | all-reduce | flops 1024 | bytes 8192 | tf_op jit(solution)/shard_map/psum | solution.py:115
  434.5 4.3 fusion.7
  438.8 188.0 %all-reduce.3.cloned.1.call-done = f32[1024,2048]{1,0:T(8,128)} async-done(((f32[1024,2048]{1,0:T(8,128)}), f32[1024,2048]{1,0:T(8,128)}) %all-reduce.3.cloned.1.call-update) | async-done | bytes 8388624
  628.3 140.6 %all-gather.9.cloned.1.call-done = f32[256,128,128]{2,1,0:T(8,128)} async-done(((f32[8,128,128]{2,1,0:T(8,128)}), f32[256,128,128]{2,1,0:T(8,128)}) %all-gather.9.cloned.1.call-update) | async-done | bytes 16777232 | tf_op jit(solution)/shard_map/all_gather | solution.py:15
  768.8 40.2 %while.31 = (s32[]{:T(128)}, f32[8,128,128]{2,1,0:T(8,128)S(1)}, s32[]{:T(128)}, f32[32,8,128,128]{3,2,1,0:T(8,128)}, s32[]{:T(128)}, /*index=5*/s32[]{:T(128)}, s32[]{:T(128)}, s32[]{:T(128)}) while((s32[]{:T(128)}, f32[8,128,128]{2,1,0:T(8,128)S(1)}, s32[]{:T(128)}, f32[32,8,128,128]{3,2,1,0:T(8,128)}, s32[]{:T(128)}, ...), condition=%wide.region_5.6_spmd.clone, body=%wide.region_4.5_spmd.clone.sunk | while | flops 393224 | bytes 1573019 | solution.py:24
  813.3 2.4 copy.54
  815.6 4.8 fusion
  820.4 2.3 copy.53
  (122 shorter events, 122.5 us)
Async XLA Ops:
  7.2 131.5 %copy-start = (bf16[1,512,2048]{2,1,0:T(8,128)(2,1)S(1)}, bf16[1,512,2048]{2,1,0:T(8,128)(2,1)}, u32[]{:S(2)}) copy-start(bf16[1,512,2048]{2,1,0:T(8,128)(2,1)} %param.13) | copy-start | bytes 6291460
  7.2 124.5 %all-gather.11.cloned.1.call-start = ((), (), s32[]{:S(2)}) async-start(), calls=%async_computation.2 | async-start | bytes 4210688 | tf_op jit(solution)/shard_map/all_gather | solution.py:73
  7.9 262.9 %all-gather.7.cloned.1.call-start = ((), (), s32[]{:S(2)}) async-start(), calls=%async_computation | async-start | bytes 17301504 | tf_op jit(solution)/shard_map/all_gather | solution.py:15
  9.5 1.5 copy-start.7
  10.9 1.6 copy-start.12
  13.8 613.0 %all-reduce.3.cloned.1.call-start = ((), (), s32[]{:S(2)}) async-start(), calls=%async_computation.3 | async-start | bytes 16777216
  13.9 2.9 copy-start.8
  15.5 1.0 copy-start.4
  15.6 1.2 copy-start.10
  338.4 3.9 copy-start.15
  338.4 3.9 copy-start.16
  350.3 1.2 copy-start.3
  350.3 1.5 copy-start.5
  350.4 418.5 %all-gather.9.cloned.1.call-start = ((), (), s32[]{:S(2)}) async-start(), calls=%async_computation.1 | async-start | bytes 17301504 | tf_op jit(solution)/shard_map/all_gather | solution.py:15
  355.2 1.6 copy-start.11
  356.8 1.4 copy-start.13
  358.2 2.5 copy-start.2
  809.1 1.8 copy-start.9
  809.1 2.7 copy-start.14
  813.3 2.4 copy-start.6
  815.6 7.0 copy-start.1
Sparse Core Ops, SparseCore 0:
  11.7 119.9 all-gather.10
  134.9 135.9 all-gather.6
  350.5 276.2 all-reduce.2
  629.3 139.5 all-gather.8
